TPU v7x, 256 devices: a whole 4x4x8 slice. The times are simulated.
256 devices in a mesh: tm: 64 (over z, x, core), col: 4 (over y).
Axes of the slice: x: 4, y: 4, z: 8, core: 2. Of those that a mesh axis runs over, the one named last changes fastest.
Arguments:
- couple: float32 [64, 1024, 1024], P('tm'), may hold values from -1 to 1
- free_term: float32 [64, 64, 1024], P('tm'), may hold values from -4 to 4
- slab_left: float32 [64, 4, 1024, 1024], P('tm', None, None, 'col'), may hold values from -0.125 to 0.125
- slab_right: float32 [64, 4, 1024, 1024], P('tm', None, None, 'col'), may hold values from -0.125 to 0.125
- arrow_rows: float32 [64, 64, 1024], P('tm', None, 'col'), may hold values from -0.0234375 to 0.0234375
- corner_base: float32 [64, 64], replicated, may hold values from -4 to 4
Outputs:
- boundary: float32 [64, 64, 1024], P('tm', None, 'col')
- slab_inverse: float32 [64, 4, 64, 1024], P('tm', None, None, 'col')
- corner: float32 [64, 64], replicated
All inputs are finite; a program needn't handle non-finite values.
Results may differ from a plain program's by a relative error of at most 0.00015.
Values sent between devices are 32-bit elements; how exact they have to be, the bound alone decides.
No kernel may reach another device: no remote copies, remote signals or barrier semaphores. Data moves between devices by JAX's collectives and lax.ppermute only.
A program may use at most 128 MiB of HBM per device.

v0:
```python
import jax
import jax.numpy as jnp
from jax import lax
from jax.sharding import PartitionSpec as P


def from_behind(array, axis, by):
    count = lax.axis_size(axis)
    pairs = [(i, i + by) for i in range(count) if 0 <= i + by < count]
    return lax.ppermute(array, axis, pairs)


def local(couple, free_term, slab_left, slab_right, arrow_rows, corner_base):
    highest = lax.Precision.HIGHEST
    transfer = couple[0]
    own_term = free_term[0]
    part_count = lax.axis_size("tm")
    col_count = lax.axis_size("col")
    col_index = lax.axis_index("col")
    col_width = transfer.shape[1] // col_count
    position = lax.axis_index("tm")

    def advance(counter, state):
        later_state = from_behind(state, "tm", -1)

        def update(incoming):
            return (
                jnp.dot(incoming, transfer, precision=highest, preferred_element_type=jnp.float32)
                + own_term
            )

        def keep_state(incoming):
            return state

        return lax.cond(part_count - 2 - position == counter, update, keep_state, later_state)

    boundary = lax.fori_loop(0, part_count - 1, advance, own_term)
    following = from_behind(boundary, "tm", -1)
    slab_blocks = jnp.einsum(
        "ab,kbc->kac", boundary, slab_left[0], precision=highest, preferred_element_type=jnp.float32
    )
    slab_blocks = slab_blocks + jnp.einsum(
        "ab,kbc->kac",
        following,
        slab_right[0],
        precision=highest,
        preferred_element_type=jnp.float32,
    )
    own_columns = lax.dynamic_slice_in_dim(boundary, col_index * col_width, col_width, 1)
    partial_value = jnp.dot(
        arrow_rows[0], own_columns.T, precision=highest, preferred_element_type=jnp.float32
    )
    corner = corner_base + lax.psum(partial_value, ("tm", "col"))
    return (own_columns[None], slab_blocks[None], corner)


def solution(mesh):
    placed = (
        P("tm", None, None),
        P("tm", None, None),
        P("tm", None, None, "col"),
        P("tm", None, None, "col"),
        P("tm", None, "col"),
        P(),
    )
    return jax.shard_map(
        local,
        mesh=mesh,
        in_specs=placed,
        out_specs=(P("tm", None, "col"), P("tm", None, None, "col"), P()),
        check_vma=False,
    )
```

profile of v0, /device:TPU:1, one launch (start us, length us, event | category | flops | bytes accessed | tf_op | source)
XLA Modules:
  0.0 790.8 jit_solution(10620637160481820337)
XLA Ops:
  1.6 669.1 %while.18 = (s32[]{:T(128)}, f32[64,1024]{1,0:T(8,128)S(1)}, s32[]{:T(128)}, f32[1024,1024]{1,0:T(8,128)}, f32[64,1024]{1,0:T(8,128)}, /*index=5*/s32[]{:T(128)}) while((s32[]{:T(128)}, f32[64,1024]{1,0:T(8,128)S(1)}, s32[]{:T(128)}, f32[1024,1024]{1,0:T(8,128)}, f32[64,1024]{1,0:T(8,128)}, /*index=5*/s32[]{:T(128)}) %tuple.60), condition=%wide.region_3.0_spmd, body=%wide.region_0.0_spmd.sunk | while | flops 805371904 | bytes 6029475 | solution.py:37
  114.0 7.9 collective-permute-done
  123.8 7.9 collective-permute-done
  133.5 7.9 collective-permute-done
  143.3 7.9 collective-permute-done
  153.1 7.9 collective-permute-done
  162.9 7.9 collective-permute-done
  172.7 7.9 collective-permute-done
  182.5 7.9 collective-permute-done
  192.3 7.9 collective-permute-done
  202.1 7.9 collective-permute-done
  211.9 7.9 collective-permute-done
  221.7 7.9 collective-permute-done
  231.4 7.9 collective-permute-done
  241.2 7.9 collective-permute-done
  251.0 7.9 collective-permute-done
  260.8 7.9 collective-permute-done
  270.6 7.9 collective-permute-done
  280.4 7.9 collective-permute-done
  290.2 7.9 collective-permute-done
  300.0 7.9 collective-permute-done
  309.8 7.9 collective-permute-done
  319.6 7.9 collective-permute-done
  329.3 7.9 collective-permute-done
  339.1 7.9 collective-permute-done
  348.9 7.9 collective-permute-done
  358.7 7.9 collective-permute-done
  368.5 7.9 collective-permute-done
  378.3 7.9 collective-permute-done
  388.1 7.9 collective-permute-done
  574.1 84.1 %collective-permute-done = f32[64,1024]{1,0:T(8,128)S(1)} collective-permute-done((f32[64,1024]{1,0:T(8,128)S(1)}, f32[64,1024]{1,0:T(8,128)S(1)}, u32[]{:S(2)}, u32[]{:S(2)}) %collective-permute-start) | collective-permute-done | bytes 262176 | tf_op jit(solution)/shard_map/while/body/eval_jaxpr/ppermute | solution.py:10
  674.2 107.5 %psum.7 = f32[64,64]{0,1:T(8,128)S(1)} all-reduce(f32[64,64]{0,1:T(8,128)S(1)} %convolution_bitcast_fusion), channel_id=1, replica_groups=mesh['tm'=64,'col'=4] {'tm','col'}, use_global_device_ids=true, to_apply=%region_4.0 | all-reduce | flops 4096 | bytes 32768 | tf_op jit(solution)/shard_map/psum | solution.py:53
  (176 shorter events, 374.3 us)
Async XLA Ops:
  112.0 9.8 %collective-permute-start = (f32[64,1024]{1,0:T(8,128)S(1)}, f32[64,1024]{1,0:T(8,128)S(1)}, u32[]{:S(2)}, u32[]{:S(2)}) collective-permute-start(f32[64,1024]{1,0:T(8,128)S(1)} %get-tuple-element.202), channel_id=1, source_target_pairs={{4,0},{8,4},{12,8},{16,12},{20,16},{24,20},{28,24},{32,28},{36,32}... | collective-permute-start | bytes 786440 | tf_op jit(solution)/shard_map/while/body/eval_jaxpr/ppermute | solution.py:10
  121.8 9.8 %collective-permute-start = (f32[64,1024]{1,0:T(8,128)S(1)}, f32[64,1024]{1,0:T(8,128)S(1)}, u32[]{:S(2)}, u32[]{:S(2)}) collective-permute-start(f32[64,1024]{1,0:T(8,128)S(1)} %get-tuple-element.202), channel_id=1, source_target_pairs={{4,0},{8,4},{12,8},{16,12},{20,16},{24,20},{28,24},{32,28},{36,32}... | collective-permute-start | bytes 786440 | tf_op jit(solution)/shard_map/while/body/eval_jaxpr/ppermute | solution.py:10
  131.6 9.8 %collective-permute-start = (f32[64,1024]{1,0:T(8,128)S(1)}, f32[64,1024]{1,0:T(8,128)S(1)}, u32[]{:S(2)}, u32[]{:S(2)}) collective-permute-start(f32[64,1024]{1,0:T(8,128)S(1)} %get-tuple-element.202), channel_id=1, source_target_pairs={{4,0},{8,4},{12,8},{16,12},{20,16},{24,20},{28,24},{32,28},{36,32}... | collective-permute-start | bytes 786440 | tf_op jit(solution)/shard_map/while/body/eval_jaxpr/ppermute | solution.py:10
  141.4 9.8 %collective-permute-start = (f32[64,1024]{1,0:T(8,128)S(1)}, f32[64,1024]{1,0:T(8,128)S(1)}, u32[]{:S(2)}, u32[]{:S(2)}) collective-permute-start(f32[64,1024]{1,0:T(8,128)S(1)} %get-tuple-element.202), channel_id=1, source_target_pairs={{4,0},{8,4},{12,8},{16,12},{20,16},{24,20},{28,24},{32,28},{36,32}... | collective-permute-start | bytes 786440 | tf_op jit(solution)/shard_map/while/body/eval_jaxpr/ppermute | solution.py:10
  151.2 9.8 %collective-permute-start = (f32[64,1024]{1,0:T(8,128)S(1)}, f32[64,1024]{1,0:T(8,128)S(1)}, u32[]{:S(2)}, u32[]{:S(2)}) collective-permute-start(f32[64,1024]{1,0:T(8,128)S(1)} %get-tuple-element.202), channel_id=1, source_target_pairs={{4,0},{8,4},{12,8},{16,12},{20,16},{24,20},{28,24},{32,28},{36,32}... | collective-permute-start | bytes 786440 | tf_op jit(solution)/shard_map/while/body/eval_jaxpr/ppermute | solution.py:10
  161.0 9.8 %collective-permute-start = (f32[64,1024]{1,0:T(8,128)S(1)}, f32[64,1024]{1,0:T(8,128)S(1)}, u32[]{:S(2)}, u32[]{:S(2)}) collective-permute-start(f32[64,1024]{1,0:T(8,128)S(1)} %get-tuple-element.202), channel_id=1, source_target_pairs={{4,0},{8,4},{12,8},{16,12},{20,16},{24,20},{28,24},{32,28},{36,32}... | collective-permute-start | bytes 786440 | tf_op jit(solution)/shard_map/while/body/eval_jaxpr/ppermute | solution.py:10
  170.8 9.8 %collective-permute-start = (f32[64,1024]{1,0:T(8,128)S(1)}, f32[64,1024]{1,0:T(8,128)S(1)}, u32[]{:S(2)}, u32[]{:S(2)}) collective-permute-start(f32[64,1024]{1,0:T(8,128)S(1)} %get-tuple-element.202), channel_id=1, source_target_pairs={{4,0},{8,4},{12,8},{16,12},{20,16},{24,20},{28,24},{32,28},{36,32}... | collective-permute-start | bytes 786440 | tf_op jit(solution)/shard_map/while/body/eval_jaxpr/ppermute | solution.py:10
  180.6 9.8 %collective-permute-start = (f32[64,1024]{1,0:T(8,128)S(1)}, f32[64,1024]{1,0:T(8,128)S(1)}, u32[]{:S(2)}, u32[]{:S(2)}) collective-permute-start(f32[64,1024]{1,0:T(8,128)S(1)} %get-tuple-element.202), channel_id=1, source_target_pairs={{4,0},{8,4},{12,8},{16,12},{20,16},{24,20},{28,24},{32,28},{36,32}... | collective-permute-start | bytes 786440 | tf_op jit(solution)/shard_map/while/body/eval_jaxpr/ppermute | solution.py:10
  190.4 9.8 %collective-permute-start = (f32[64,1024]{1,0:T(8,128)S(1)}, f32[64,1024]{1,0:T(8,128)S(1)}, u32[]{:S(2)}, u32[]{:S(2)}) collective-permute-start(f32[64,1024]{1,0:T(8,128)S(1)} %get-tuple-element.202), channel_id=1, source_target_pairs={{4,0},{8,4},{12,8},{16,12},{20,16},{24,20},{28,24},{32,28},{36,32}... | collective-permute-start | bytes 786440 | tf_op jit(solution)/shard_map/while/body/eval_jaxpr/ppermute | solution.py:10
  200.2 9.8 %collective-permute-start = (f32[64,1024]{1,0:T(8,128)S(1)}, f32[64,1024]{1,0:T(8,128)S(1)}, u32[]{:S(2)}, u32[]{:S(2)}) collective-permute-start(f32[64,1024]{1,0:T(8,128)S(1)} %get-tuple-element.202), channel_id=1, source_target_pairs={{4,0},{8,4},{12,8},{16,12},{20,16},{24,20},{28,24},{32,28},{36,32}... | collective-permute-start | bytes 786440 | tf_op jit(solution)/shard_map/while/body/eval_jaxpr/ppermute | solution.py:10
  209.9 9.8 %collective-permute-start = (f32[64,1024]{1,0:T(8,128)S(1)}, f32[64,1024]{1,0:T(8,128)S(1)}, u32[]{:S(2)}, u32[]{:S(2)}) collective-permute-start(f32[64,1024]{1,0:T(8,128)S(1)} %get-tuple-element.202), channel_id=1, source_target_pairs={{4,0},{8,4},{12,8},{16,12},{20,16},{24,20},{28,24},{32,28},{36,32}... | collective-permute-start | bytes 786440 | tf_op jit(solution)/shard_map/while/body/eval_jaxpr/ppermute | solution.py:10
  219.7 9.8 %collective-permute-start = (f32[64,1024]{1,0:T(8,128)S(1)}, f32[64,1024]{1,0:T(8,128)S(1)}, u32[]{:S(2)}, u32[]{:S(2)}) collective-permute-start(f32[64,1024]{1,0:T(8,128)S(1)} %get-tuple-element.202), channel_id=1, source_target_pairs={{4,0},{8,4},{12,8},{16,12},{20,16},{24,20},{28,24},{32,28},{36,32}... | collective-permute-start | bytes 786440 | tf_op jit(solution)/shard_map/while/body/eval_jaxpr/ppermute | solution.py:10
  229.5 9.8 %collective-permute-start = (f32[64,1024]{1,0:T(8,128)S(1)}, f32[64,1024]{1,0:T(8,128)S(1)}, u32[]{:S(2)}, u32[]{:S(2)}) collective-permute-start(f32[64,1024]{1,0:T(8,128)S(1)} %get-tuple-element.202), channel_id=1, source_target_pairs={{4,0},{8,4},{12,8},{16,12},{20,16},{24,20},{28,24},{32,28},{36,32}... | collective-permute-start | bytes 786440 | tf_op jit(solution)/shard_map/while/body/eval_jaxpr/ppermute | solution.py:10
  239.3 9.8 %collective-permute-start = (f32[64,1024]{1,0:T(8,128)S(1)}, f32[64,1024]{1,0:T(8,128)S(1)}, u32[]{:S(2)}, u32[]{:S(2)}) collective-permute-start(f32[64,1024]{1,0:T(8,128)S(1)} %get-tuple-element.202), channel_id=1, source_target_pairs={{4,0},{8,4},{12,8},{16,12},{20,16},{24,20},{28,24},{32,28},{36,32}... | collective-permute-start | bytes 786440 | tf_op jit(solution)/shard_map/while/body/eval_jaxpr/ppermute | solution.py:10
  249.1 9.8 %collective-permute-start = (f32[64,1024]{1,0:T(8,128)S(1)}, f32[64,1024]{1,0:T(8,128)S(1)}, u32[]{:S(2)}, u32[]{:S(2)}) collective-permute-start(f32[64,1024]{1,0:T(8,128)S(1)} %get-tuple-element.202), channel_id=1, source_target_pairs={{4,0},{8,4},{12,8},{16,12},{20,16},{24,20},{28,24},{32,28},{36,32}... | collective-permute-start | bytes 786440 | tf_op jit(solution)/shard_map/while/body/eval_jaxpr/ppermute | solution.py:10
  258.9 9.8 %collective-permute-start = (f32[64,1024]{1,0:T(8,128)S(1)}, f32[64,1024]{1,0:T(8,128)S(1)}, u32[]{:S(2)}, u32[]{:S(2)}) collective-permute-start(f32[64,1024]{1,0:T(8,128)S(1)} %get-tuple-element.202), channel_id=1, source_target_pairs={{4,0},{8,4},{12,8},{16,12},{20,16},{24,20},{28,24},{32,28},{36,32}... | collective-permute-start | bytes 786440 | tf_op jit(solution)/shard_map/while/body/eval_jaxpr/ppermute | solution.py:10
  268.7 9.8 %collective-permute-start = (f32[64,1024]{1,0:T(8,128)S(1)}, f32[64,1024]{1,0:T(8,128)S(1)}, u32[]{:S(2)}, u32[]{:S(2)}) collective-permute-start(f32[64,1024]{1,0:T(8,128)S(1)} %get-tuple-element.202), channel_id=1, source_target_pairs={{4,0},{8,4},{12,8},{16,12},{20,16},{24,20},{28,24},{32,28},{36,32}... | collective-permute-start | bytes 786440 | tf_op jit(solution)/shard_map/while/body/eval_jaxpr/ppermute | solution.py:10
  278.5 9.8 %collective-permute-start = (f32[64,1024]{1,0:T(8,128)S(1)}, f32[64,1024]{1,0:T(8,128)S(1)}, u32[]{:S(2)}, u32[]{:S(2)}) collective-permute-start(f32[64,1024]{1,0:T(8,128)S(1)} %get-tuple-element.202), channel_id=1, source_target_pairs={{4,0},{8,4},{12,8},{16,12},{20,16},{24,20},{28,24},{32,28},{36,32}... | collective-permute-start | bytes 786440 | tf_op jit(solution)/shard_map/while/body/eval_jaxpr/ppermute | solution.py:10
  288.3 9.8 %collective-permute-start = (f32[64,1024]{1,0:T(8,128)S(1)}, f32[64,1024]{1,0:T(8,128)S(1)}, u32[]{:S(2)}, u32[]{:S(2)}) collective-permute-start(f32[64,1024]{1,0:T(8,128)S(1)} %get-tuple-element.202), channel_id=1, source_target_pairs={{4,0},{8,4},{12,8},{16,12},{20,16},{24,20},{28,24},{32,28},{36,32}... | collective-permute-start | bytes 786440 | tf_op jit(solution)/shard_map/while/body/eval_jaxpr/ppermute | solution.py:10
  298.1 9.8 %collective-permute-start = (f32[64,1024]{1,0:T(8,128)S(1)}, f32[64,1024]{1,0:T(8,128)S(1)}, u32[]{:S(2)}, u32[]{:S(2)}) collective-permute-start(f32[64,1024]{1,0:T(8,128)S(1)} %get-tuple-element.202), channel_id=1, source_target_pairs={{4,0},{8,4},{12,8},{16,12},{20,16},{24,20},{28,24},{32,28},{36,32}... | collective-permute-start | bytes 786440 | tf_op jit(solution)/shard_map/while/body/eval_jaxpr/ppermute | solution.py:10
  307.8 9.8 %collective-permute-start = (f32[64,1024]{1,0:T(8,128)S(1)}, f32[64,1024]{1,0:T(8,128)S(1)}, u32[]{:S(2)}, u32[]{:S(2)}) collective-permute-start(f32[64,1024]{1,0:T(8,128)S(1)} %get-tuple-element.202), channel_id=1, source_target_pairs={{4,0},{8,4},{12,8},{16,12},{20,16},{24,20},{28,24},{32,28},{36,32}... | collective-permute-start | bytes 786440 | tf_op jit(solution)/shard_map/while/body/eval_jaxpr/ppermute | solution.py:10
  317.6 9.8 %collective-permute-start = (f32[64,1024]{1,0:T(8,128)S(1)}, f32[64,1024]{1,0:T(8,128)S(1)}, u32[]{:S(2)}, u32[]{:S(2)}) collective-permute-start(f32[64,1024]{1,0:T(8,128)S(1)} %get-tuple-element.202), channel_id=1, source_target_pairs={{4,0},{8,4},{12,8},{16,12},{20,16},{24,20},{28,24},{32,28},{36,32}... | collective-permute-start | bytes 786440 | tf_op jit(solution)/shard_map/while/body/eval_jaxpr/ppermute | solution.py:10
  327.4 9.8 %collective-permute-start = (f32[64,1024]{1,0:T(8,128)S(1)}, f32[64,1024]{1,0:T(8,128)S(1)}, u32[]{:S(2)}, u32[]{:S(2)}) collective-permute-start(f32[64,1024]{1,0:T(8,128)S(1)} %get-tuple-element.202), channel_id=1, source_target_pairs={{4,0},{8,4},{12,8},{16,12},{20,16},{24,20},{28,24},{32,28},{36,32}... | collective-permute-start | bytes 786440 | tf_op jit(solution)/shard_map/while/body/eval_jaxpr/ppermute | solution.py:10
  337.2 9.8 %collective-permute-start = (f32[64,1024]{1,0:T(8,128)S(1)}, f32[64,1024]{1,0:T(8,128)S(1)}, u32[]{:S(2)}, u32[]{:S(2)}) collective-permute-start(f32[64,1024]{1,0:T(8,128)S(1)} %get-tuple-element.202), channel_id=1, source_target_pairs={{4,0},{8,4},{12,8},{16,12},{20,16},{24,20},{28,24},{32,28},{36,32}... | collective-permute-start | bytes 786440 | tf_op jit(solution)/shard_map/while/body/eval_jaxpr/ppermute | solution.py:10
  347.0 9.8 %collective-permute-start = (f32[64,1024]{1,0:T(8,128)S(1)}, f32[64,1024]{1,0:T(8,128)S(1)}, u32[]{:S(2)}, u32[]{:S(2)}) collective-permute-start(f32[64,1024]{1,0:T(8,128)S(1)} %get-tuple-element.202), channel_id=1, source_target_pairs={{4,0},{8,4},{12,8},{16,12},{20,16},{24,20},{28,24},{32,28},{36,32}... | collective-permute-start | bytes 786440 | tf_op jit(solution)/shard_map/while/body/eval_jaxpr/ppermute | solution.py:10
  356.8 9.8 %collective-permute-start = (f32[64,1024]{1,0:T(8,128)S(1)}, f32[64,1024]{1,0:T(8,128)S(1)}, u32[]{:S(2)}, u32[]{:S(2)}) collective-permute-start(f32[64,1024]{1,0:T(8,128)S(1)} %get-tuple-element.202), channel_id=1, source_target_pairs={{4,0},{8,4},{12,8},{16,12},{20,16},{24,20},{28,24},{32,28},{36,32}... | collective-permute-start | bytes 786440 | tf_op jit(solution)/shard_map/while/body/eval_jaxpr/ppermute | solution.py:10
  366.6 9.8 %collective-permute-start = (f32[64,1024]{1,0:T(8,128)S(1)}, f32[64,1024]{1,0:T(8,128)S(1)}, u32[]{:S(2)}, u32[]{:S(2)}) collective-permute-start(f32[64,1024]{1,0:T(8,128)S(1)} %get-tuple-element.202), channel_id=1, source_target_pairs={{4,0},{8,4},{12,8},{16,12},{20,16},{24,20},{28,24},{32,28},{36,32}... | collective-permute-start | bytes 786440 | tf_op jit(solution)/shard_map/while/body/eval_jaxpr/ppermute | solution.py:10
  376.4 9.8 %collective-permute-start = (f32[64,1024]{1,0:T(8,128)S(1)}, f32[64,1024]{1,0:T(8,128)S(1)}, u32[]{:S(2)}, u32[]{:S(2)}) collective-permute-start(f32[64,1024]{1,0:T(8,128)S(1)} %get-tuple-element.202), channel_id=1, source_target_pairs={{4,0},{8,4},{12,8},{16,12},{20,16},{24,20},{28,24},{32,28},{36,32}... | collective-permute-start | bytes 786440 | tf_op jit(solution)/shard_map/while/body/eval_jaxpr/ppermute | solution.py:10
  386.2 9.8 %collective-permute-start = (f32[64,1024]{1,0:T(8,128)S(1)}, f32[64,1024]{1,0:T(8,128)S(1)}, u32[]{:S(2)}, u32[]{:S(2)}) collective-permute-start(f32[64,1024]{1,0:T(8,128)S(1)} %get-tuple-element.202), channel_id=1, source_target_pairs={{4,0},{8,4},{12,8},{16,12},{20,16},{24,20},{28,24},{32,28},{36,32}... | collective-permute-start | bytes 786440 | tf_op jit(solution)/shard_map/while/body/eval_jaxpr/ppermute | solution.py:10
  396.0 9.8 %collective-permute-start = (f32[64,1024]{1,0:T(8,128)S(1)}, f32[64,1024]{1,0:T(8,128)S(1)}, u32[]{:S(2)}, u32[]{:S(2)}) collective-permute-start(f32[64,1024]{1,0:T(8,128)S(1)} %get-tuple-element.202), channel_id=1, source_target_pairs={{4,0},{8,4},{12,8},{16,12},{20,16},{24,20},{28,24},{32,28},{36,32}... | collective-permute-start | bytes 786440 | tf_op jit(solution)/shard_map/while/body/eval_jaxpr/ppermute | solution.py:10
  572.2 86.0 %collective-permute-start = (f32[64,1024]{1,0:T(8,128)S(1)}, f32[64,1024]{1,0:T(8,128)S(1)}, u32[]{:S(2)}, u32[]{:S(2)}) collective-permute-start(f32[64,1024]{1,0:T(8,128)S(1)} %get-tuple-element.202), channel_id=1, source_target_pairs={{4,0},{8,4},{12,8},{16,12},{20,16},{24,20},{28,24},{32,28},{36,32}... | collective-permute-start | bytes 786440 | tf_op jit(solution)/shard_map/while/body/eval_jaxpr/ppermute | solution.py:10
  670.7 116.7 %collective-permute-start.1 = (f32[64,1024]{1,0:T(8,128)S(1)}, f32[64,1024]{1,0:T(8,128)S(1)}, u32[]{:S(2)}, u32[]{:S(2)}) collective-permute-start(f32[64,1024]{1,0:T(8,128)S(1)} %get-tuple-element.150), channel_id=1, source_target_pairs={{4,0},{8,4},{12,8},{16,12},{20,16},{24,20},{28,24},{32,28},{36,32}... | collective-permute-start | bytes 786440 | tf_op jit(solution)/shard_map/ppermute | solution.py:10
  (35 other events, 1635.1 us)
where the time goes:
time: 793 us; the launch traced here: 791 us
  waiting for transfers between devices  540 us (68%)
  starting transfers between devices  126 us (16%)
  blocking collectives  108 us (14%)
  matrix products  13.4 us (2%)
    ppermute x64, waiting for transfers between devices, from_behind(): return lax.ppermute(array, axis, pairs)  540 us
    ppermute x64, starting transfers between devices, from_behind(): return lax.ppermute(array, axis, pairs)  126 us
    psum x1, blocking collectives, local(): corner = corner_base + lax.psum(partial_value, ('tm', 'col'))  108 us
  transfers between devices with their start and end apart: 64, of which 63 were waited for; matrix products, arithmetic and copies ran while one was open for 1% of the time, Pallas kernels for 0%

commit v1 on v0

--- a/solution.py
+++ b/solution.py
@@ -11,6 +11,11 @@
 
 
 def local(couple, free_term, slab_left, slab_right, arrow_rows, corner_base):
+
+    def ways_settle(sample, ax_name):
+        ready = lax.all_gather(sample, ax_name)
+        return jnp.sum(ready, axis=0)
+
     highest = lax.Precision.HIGHEST
     transfer = couple[0]
     own_term = free_term[0]
@@ -50,7 +55,7 @@
     partial_value = jnp.dot(
         arrow_rows[0], own_columns.T, precision=highest, preferred_element_type=jnp.float32
     )
-    corner = corner_base + lax.psum(partial_value, ("tm", "col"))
+    corner = corner_base + ways_settle(partial_value, ("tm", "col"))
     return (own_columns[None], slab_blocks[None], corner)
 
 

time: 793 us -> 840 us (1.059)
  waiting for transfers between devices: 540 us -> 676 us
  blocking collectives: 108 us -> 0 us
  between operations: 0.7 us -> 14.1 us
    all_gather x0 -> x1, waiting for transfers between devices: none -> 136 us  [ways_settle(): ready = lax.all_gather(sample, ax_name)]
    psum x1 -> x0, blocking collectives: 108 us -> none  [local(): corner = corner_base + lax.psum(partial_value, ('tm', 'col'))]
  transfers between devices with their start and end apart: 64 -> 65, of which waited for: 63 -> 64; matrix products, arithmetic and copies ran while one was open for 1% -> 1% of each run, Pallas kernels for 0% -> 0%
where the time goes in v1:
time: 840 us; the launch traced here: 838 us
  waiting for transfers between devices  676 us (80%)
  starting transfers between devices  126 us (15%)
  between operations  14.1 us (2%)
  matrix products  13.6 us (2%)
    ppermute x64, waiting for transfers between devices, from_behind(): return lax.ppermute(array, axis, pairs)  540 us
    all_gather x1, waiting for transfers between devices, ways_settle(): ready = lax.all_gather(sample, ax_name)  136 us
    ppermute x64, starting transfers between devices, from_behind(): return lax.ppermute(array, axis, pairs)  126 us
  transfers between devices with their start and end apart: 65, of which 64 were waited for; matrix products, arithmetic and copies ran while one was open for 1% of the time, Pallas kernels for 0%

profile of v1, /device:TPU:1, one launch (start us, length us, event | category | flops | bytes accessed | tf_op | source)
XLA Modules:
  0.0 838.1 jit_solution(9417791552201935555)
XLA Ops:
  8.2 669.1 %while.18 = (s32[]{:T(128)}, f32[64,1024]{1,0:T(8,128)S(1)}, s32[]{:T(128)}, f32[1024,1024]{1,0:T(8,128)}, f32[64,1024]{1,0:T(8,128)}, /*index=5*/s32[]{:T(128)}) while((s32[]{:T(128)}, f32[64,1024]{1,0:T(8,128)S(1)}, s32[]{:T(128)}, f32[1024,1024]{1,0:T(8,128)}, f32[64,1024]{1,0:T(8,128)}, /*index=5*/s32[]{:T(128)}) %tuple.62), condition=%wide.region_3.0_spmd, body=%wide.region_0.0_spmd.sunk | while | flops 805371904 | bytes 6029467 | solution.py:42
  120.5 7.9 collective-permute-done
  130.3 7.9 collective-permute-done
  140.1 7.9 collective-permute-done
  149.9 7.9 collective-permute-done
  159.7 7.9 collective-permute-done
  169.5 7.9 collective-permute-done
  179.3 7.9 collective-permute-done
  189.0 7.9 collective-permute-done
  198.8 7.9 collective-permute-done
  208.6 7.9 collective-permute-done
  218.4 7.9 collective-permute-done
  228.2 7.9 collective-permute-done
  238.0 7.9 collective-permute-done
  247.8 7.9 collective-permute-done
  257.6 7.9 collective-permute-done
  267.4 7.9 collective-permute-done
  277.2 7.9 collective-permute-done
  286.9 7.9 collective-permute-done
  296.7 7.9 collective-permute-done
  306.5 7.9 collective-permute-done
  316.3 7.9 collective-permute-done
  326.1 7.9 collective-permute-done
  335.9 7.9 collective-permute-done
  345.7 7.9 collective-permute-done
  355.5 7.9 collective-permute-done
  365.3 7.9 collective-permute-done
  375.1 7.9 collective-permute-done
  384.8 7.9 collective-permute-done
  394.6 7.9 collective-permute-done
  580.6 84.1 %collective-permute-done = f32[64,1024]{1,0:T(8,128)S(1)} collective-permute-done((f32[64,1024]{1,0:T(8,128)S(1)}, f32[64,1024]{1,0:T(8,128)S(1)}, u32[]{:S(2)}, u32[]{:S(2)}) %collective-permute-start) | collective-permute-done | bytes 262176 | tf_op jit(solution)/shard_map/while/body/eval_jaxpr/ppermute | solution.py:10
  690.1 136.4 %all-gather.3.cloned.1.call-done = f32[16384,64]{1,0:T(8,128)} async-done(((f32[64,64]{1,0:T(8,128)}), f32[16384,64]{1,0:T(8,128)}) %all-gather.3.cloned.1.call-update) | async-done | bytes 4194320 | tf_op jit(solution)/shard_map/all_gather | solution.py:16
  (181 shorter events, 379.3 us)
Async XLA Ops:
  7.2 819.3 %all-gather.3.cloned.1.call-start = ((), (), s32[]{:S(2)}) async-start(), calls=%async_computation | async-start | bytes 8421376 | tf_op jit(solution)/shard_map/all_gather | solution.py:16
  118.6 9.8 %collective-permute-start = (f32[64,1024]{1,0:T(8,128)S(1)}, f32[64,1024]{1,0:T(8,128)S(1)}, u32[]{:S(2)}, u32[]{:S(2)}) collective-permute-start(f32[64,1024]{1,0:T(8,128)S(1)} %get-tuple-element.202), channel_id=1, source_target_pairs={{4,0},{8,4},{12,8},{16,12},{20,16},{24,20},{28,24},{32,28},{36,32}... | collective-permute-start | bytes 786440 | tf_op jit(solution)/shard_map/while/body/eval_jaxpr/ppermute | solution.py:10
  128.4 9.8 %collective-permute-start = (f32[64,1024]{1,0:T(8,128)S(1)}, f32[64,1024]{1,0:T(8,128)S(1)}, u32[]{:S(2)}, u32[]{:S(2)}) collective-permute-start(f32[64,1024]{1,0:T(8,128)S(1)} %get-tuple-element.202), channel_id=1, source_target_pairs={{4,0},{8,4},{12,8},{16,12},{20,16},{24,20},{28,24},{32,28},{36,32}... | collective-permute-start | bytes 786440 | tf_op jit(solution)/shard_map/while/body/eval_jaxpr/ppermute | solution.py:10
  138.2 9.8 %collective-permute-start = (f32[64,1024]{1,0:T(8,128)S(1)}, f32[64,1024]{1,0:T(8,128)S(1)}, u32[]{:S(2)}, u32[]{:S(2)}) collective-permute-start(f32[64,1024]{1,0:T(8,128)S(1)} %get-tuple-element.202), channel_id=1, source_target_pairs={{4,0},{8,4},{12,8},{16,12},{20,16},{24,20},{28,24},{32,28},{36,32}... | collective-permute-start | bytes 786440 | tf_op jit(solution)/shard_map/while/body/eval_jaxpr/ppermute | solution.py:10
  148.0 9.8 %collective-permute-start = (f32[64,1024]{1,0:T(8,128)S(1)}, f32[64,1024]{1,0:T(8,128)S(1)}, u32[]{:S(2)}, u32[]{:S(2)}) collective-permute-start(f32[64,1024]{1,0:T(8,128)S(1)} %get-tuple-element.202), channel_id=1, source_target_pairs={{4,0},{8,4},{12,8},{16,12},{20,16},{24,20},{28,24},{32,28},{36,32}... | collective-permute-start | bytes 786440 | tf_op jit(solution)/shard_map/while/body/eval_jaxpr/ppermute | solution.py:10
  157.8 9.8 %collective-permute-start = (f32[64,1024]{1,0:T(8,128)S(1)}, f32[64,1024]{1,0:T(8,128)S(1)}, u32[]{:S(2)}, u32[]{:S(2)}) collective-permute-start(f32[64,1024]{1,0:T(8,128)S(1)} %get-tuple-element.202), channel_id=1, source_target_pairs={{4,0},{8,4},{12,8},{16,12},{20,16},{24,20},{28,24},{32,28},{36,32}... | collective-permute-start | bytes 786440 | tf_op jit(solution)/shard_map/while/body/eval_jaxpr/ppermute | solution.py:10
  167.5 9.8 %collective-permute-start = (f32[64,1024]{1,0:T(8,128)S(1)}, f32[64,1024]{1,0:T(8,128)S(1)}, u32[]{:S(2)}, u32[]{:S(2)}) collective-permute-start(f32[64,1024]{1,0:T(8,128)S(1)} %get-tuple-element.202), channel_id=1, source_target_pairs={{4,0},{8,4},{12,8},{16,12},{20,16},{24,20},{28,24},{32,28},{36,32}... | collective-permute-start | bytes 786440 | tf_op jit(solution)/shard_map/while/body/eval_jaxpr/ppermute | solution.py:10
  177.3 9.8 %collective-permute-start = (f32[64,1024]{1,0:T(8,128)S(1)}, f32[64,1024]{1,0:T(8,128)S(1)}, u32[]{:S(2)}, u32[]{:S(2)}) collective-permute-start(f32[64,1024]{1,0:T(8,128)S(1)} %get-tuple-element.202), channel_id=1, source_target_pairs={{4,0},{8,4},{12,8},{16,12},{20,16},{24,20},{28,24},{32,28},{36,32}... | collective-permute-start | bytes 786440 | tf_op jit(solution)/shard_map/while/body/eval_jaxpr/ppermute | solution.py:10
  187.1 9.8 %collective-permute-start = (f32[64,1024]{1,0:T(8,128)S(1)}, f32[64,1024]{1,0:T(8,128)S(1)}, u32[]{:S(2)}, u32[]{:S(2)}) collective-permute-start(f32[64,1024]{1,0:T(8,128)S(1)} %get-tuple-element.202), channel_id=1, source_target_pairs={{4,0},{8,4},{12,8},{16,12},{20,16},{24,20},{28,24},{32,28},{36,32}... | collective-permute-start | bytes 786440 | tf_op jit(solution)/shard_map/while/body/eval_jaxpr/ppermute | solution.py:10
  196.9 9.8 %collective-permute-start = (f32[64,1024]{1,0:T(8,128)S(1)}, f32[64,1024]{1,0:T(8,128)S(1)}, u32[]{:S(2)}, u32[]{:S(2)}) collective-permute-start(f32[64,1024]{1,0:T(8,128)S(1)} %get-tuple-element.202), channel_id=1, source_target_pairs={{4,0},{8,4},{12,8},{16,12},{20,16},{24,20},{28,24},{32,28},{36,32}... | collective-permute-start | bytes 786440 | tf_op jit(solution)/shard_map/while/body/eval_jaxpr/ppermute | solution.py:10
  206.7 9.8 %collective-permute-start = (f32[64,1024]{1,0:T(8,128)S(1)}, f32[64,1024]{1,0:T(8,128)S(1)}, u32[]{:S(2)}, u32[]{:S(2)}) collective-permute-start(f32[64,1024]{1,0:T(8,128)S(1)} %get-tuple-element.202), channel_id=1, source_target_pairs={{4,0},{8,4},{12,8},{16,12},{20,16},{24,20},{28,24},{32,28},{36,32}... | collective-permute-start | bytes 786440 | tf_op jit(solution)/shard_map/while/body/eval_jaxpr/ppermute | solution.py:10
  216.5 9.8 %collective-permute-start = (f32[64,1024]{1,0:T(8,128)S(1)}, f32[64,1024]{1,0:T(8,128)S(1)}, u32[]{:S(2)}, u32[]{:S(2)}) collective-permute-start(f32[64,1024]{1,0:T(8,128)S(1)} %get-tuple-element.202), channel_id=1, source_target_pairs={{4,0},{8,4},{12,8},{16,12},{20,16},{24,20},{28,24},{32,28},{36,32}... | collective-permute-start | bytes 786440 | tf_op jit(solution)/shard_map/while/body/eval_jaxpr/ppermute | solution.py:10
  226.3 9.8 %collective-permute-start = (f32[64,1024]{1,0:T(8,128)S(1)}, f32[64,1024]{1,0:T(8,128)S(1)}, u32[]{:S(2)}, u32[]{:S(2)}) collective-permute-start(f32[64,1024]{1,0:T(8,128)S(1)} %get-tuple-element.202), channel_id=1, source_target_pairs={{4,0},{8,4},{12,8},{16,12},{20,16},{24,20},{28,24},{32,28},{36,32}... | collective-permute-start | bytes 786440 | tf_op jit(solution)/shard_map/while/body/eval_jaxpr/ppermute | solution.py:10
  236.1 9.8 %collective-permute-start = (f32[64,1024]{1,0:T(8,128)S(1)}, f32[64,1024]{1,0:T(8,128)S(1)}, u32[]{:S(2)}, u32[]{:S(2)}) collective-permute-start(f32[64,1024]{1,0:T(8,128)S(1)} %get-tuple-element.202), channel_id=1, source_target_pairs={{4,0},{8,4},{12,8},{16,12},{20,16},{24,20},{28,24},{32,28},{36,32}... | collective-permute-start | bytes 786440 | tf_op jit(solution)/shard_map/while/body/eval_jaxpr/ppermute | solution.py:10
  245.9 9.8 %collective-permute-start = (f32[64,1024]{1,0:T(8,128)S(1)}, f32[64,1024]{1,0:T(8,128)S(1)}, u32[]{:S(2)}, u32[]{:S(2)}) collective-permute-start(f32[64,1024]{1,0:T(8,128)S(1)} %get-tuple-element.202), channel_id=1, source_target_pairs={{4,0},{8,4},{12,8},{16,12},{20,16},{24,20},{28,24},{32,28},{36,32}... | collective-permute-start | bytes 786440 | tf_op jit(solution)/shard_map/while/body/eval_jaxpr/ppermute | solution.py:10
  255.7 9.8 %collective-permute-start = (f32[64,1024]{1,0:T(8,128)S(1)}, f32[64,1024]{1,0:T(8,128)S(1)}, u32[]{:S(2)}, u32[]{:S(2)}) collective-permute-start(f32[64,1024]{1,0:T(8,128)S(1)} %get-tuple-element.202), channel_id=1, source_target_pairs={{4,0},{8,4},{12,8},{16,12},{20,16},{24,20},{28,24},{32,28},{36,32}... | collective-permute-start | bytes 786440 | tf_op jit(solution)/shard_map/while/body/eval_jaxpr/ppermute | solution.py:10
  265.4 9.8 %collective-permute-start = (f32[64,1024]{1,0:T(8,128)S(1)}, f32[64,1024]{1,0:T(8,128)S(1)}, u32[]{:S(2)}, u32[]{:S(2)}) collective-permute-start(f32[64,1024]{1,0:T(8,128)S(1)} %get-tuple-element.202), channel_id=1, source_target_pairs={{4,0},{8,4},{12,8},{16,12},{20,16},{24,20},{28,24},{32,28},{36,32}... | collective-permute-start | bytes 786440 | tf_op jit(solution)/shard_map/while/body/eval_jaxpr/ppermute | solution.py:10
  275.2 9.8 %collective-permute-start = (f32[64,1024]{1,0:T(8,128)S(1)}, f32[64,1024]{1,0:T(8,128)S(1)}, u32[]{:S(2)}, u32[]{:S(2)}) collective-permute-start(f32[64,1024]{1,0:T(8,128)S(1)} %get-tuple-element.202), channel_id=1, source_target_pairs={{4,0},{8,4},{12,8},{16,12},{20,16},{24,20},{28,24},{32,28},{36,32}... | collective-permute-start | bytes 786440 | tf_op jit(solution)/shard_map/while/body/eval_jaxpr/ppermute | solution.py:10
  285.0 9.8 %collective-permute-start = (f32[64,1024]{1,0:T(8,128)S(1)}, f32[64,1024]{1,0:T(8,128)S(1)}, u32[]{:S(2)}, u32[]{:S(2)}) collective-permute-start(f32[64,1024]{1,0:T(8,128)S(1)} %get-tuple-element.202), channel_id=1, source_target_pairs={{4,0},{8,4},{12,8},{16,12},{20,16},{24,20},{28,24},{32,28},{36,32}... | collective-permute-start | bytes 786440 | tf_op jit(solution)/shard_map/while/body/eval_jaxpr/ppermute | solution.py:10
  294.8 9.8 %collective-permute-start = (f32[64,1024]{1,0:T(8,128)S(1)}, f32[64,1024]{1,0:T(8,128)S(1)}, u32[]{:S(2)}, u32[]{:S(2)}) collective-permute-start(f32[64,1024]{1,0:T(8,128)S(1)} %get-tuple-element.202), channel_id=1, source_target_pairs={{4,0},{8,4},{12,8},{16,12},{20,16},{24,20},{28,24},{32,28},{36,32}... | collective-permute-start | bytes 786440 | tf_op jit(solution)/shard_map/while/body/eval_jaxpr/ppermute | solution.py:10
  304.6 9.8 %collective-permute-start = (f32[64,1024]{1,0:T(8,128)S(1)}, f32[64,1024]{1,0:T(8,128)S(1)}, u32[]{:S(2)}, u32[]{:S(2)}) collective-permute-start(f32[64,1024]{1,0:T(8,128)S(1)} %get-tuple-element.202), channel_id=1, source_target_pairs={{4,0},{8,4},{12,8},{16,12},{20,16},{24,20},{28,24},{32,28},{36,32}... | collective-permute-start | bytes 786440 | tf_op jit(solution)/shard_map/while/body/eval_jaxpr/ppermute | solution.py:10
  314.4 9.8 %collective-permute-start = (f32[64,1024]{1,0:T(8,128)S(1)}, f32[64,1024]{1,0:T(8,128)S(1)}, u32[]{:S(2)}, u32[]{:S(2)}) collective-permute-start(f32[64,1024]{1,0:T(8,128)S(1)} %get-tuple-element.202), channel_id=1, source_target_pairs={{4,0},{8,4},{12,8},{16,12},{20,16},{24,20},{28,24},{32,28},{36,32}... | collective-permute-start | bytes 786440 | tf_op jit(solution)/shard_map/while/body/eval_jaxpr/ppermute | solution.py:10
  324.2 9.8 %collective-permute-start = (f32[64,1024]{1,0:T(8,128)S(1)}, f32[64,1024]{1,0:T(8,128)S(1)}, u32[]{:S(2)}, u32[]{:S(2)}) collective-permute-start(f32[64,1024]{1,0:T(8,128)S(1)} %get-tuple-element.202), channel_id=1, source_target_pairs={{4,0},{8,4},{12,8},{16,12},{20,16},{24,20},{28,24},{32,28},{36,32}... | collective-permute-start | bytes 786440 | tf_op jit(solution)/shard_map/while/body/eval_jaxpr/ppermute | solution.py:10
  334.0 9.8 %collective-permute-start = (f32[64,1024]{1,0:T(8,128)S(1)}, f32[64,1024]{1,0:T(8,128)S(1)}, u32[]{:S(2)}, u32[]{:S(2)}) collective-permute-start(f32[64,1024]{1,0:T(8,128)S(1)} %get-tuple-element.202), channel_id=1, source_target_pairs={{4,0},{8,4},{12,8},{16,12},{20,16},{24,20},{28,24},{32,28},{36,32}... | collective-permute-start | bytes 786440 | tf_op jit(solution)/shard_map/while/body/eval_jaxpr/ppermute | solution.py:10
  343.8 9.8 %collective-permute-start = (f32[64,1024]{1,0:T(8,128)S(1)}, f32[64,1024]{1,0:T(8,128)S(1)}, u32[]{:S(2)}, u32[]{:S(2)}) collective-permute-start(f32[64,1024]{1,0:T(8,128)S(1)} %get-tuple-element.202), channel_id=1, source_target_pairs={{4,0},{8,4},{12,8},{16,12},{20,16},{24,20},{28,24},{32,28},{36,32}... | collective-permute-start | bytes 786440 | tf_op jit(solution)/shard_map/while/body/eval_jaxpr/ppermute | solution.py:10
  353.6 9.8 %collective-permute-start = (f32[64,1024]{1,0:T(8,128)S(1)}, f32[64,1024]{1,0:T(8,128)S(1)}, u32[]{:S(2)}, u32[]{:S(2)}) collective-permute-start(f32[64,1024]{1,0:T(8,128)S(1)} %get-tuple-element.202), channel_id=1, source_target_pairs={{4,0},{8,4},{12,8},{16,12},{20,16},{24,20},{28,24},{32,28},{36,32}... | collective-permute-start | bytes 786440 | tf_op jit(solution)/shard_map/while/body/eval_jaxpr/ppermute | solution.py:10
  363.3 9.8 %collective-permute-start = (f32[64,1024]{1,0:T(8,128)S(1)}, f32[64,1024]{1,0:T(8,128)S(1)}, u32[]{:S(2)}, u32[]{:S(2)}) collective-permute-start(f32[64,1024]{1,0:T(8,128)S(1)} %get-tuple-element.202), channel_id=1, source_target_pairs={{4,0},{8,4},{12,8},{16,12},{20,16},{24,20},{28,24},{32,28},{36,32}... | collective-permute-start | bytes 786440 | tf_op jit(solution)/shard_map/while/body/eval_jaxpr/ppermute | solution.py:10
  373.1 9.8 %collective-permute-start = (f32[64,1024]{1,0:T(8,128)S(1)}, f32[64,1024]{1,0:T(8,128)S(1)}, u32[]{:S(2)}, u32[]{:S(2)}) collective-permute-start(f32[64,1024]{1,0:T(8,128)S(1)} %get-tuple-element.202), channel_id=1, source_target_pairs={{4,0},{8,4},{12,8},{16,12},{20,16},{24,20},{28,24},{32,28},{36,32}... | collective-permute-start | bytes 786440 | tf_op jit(solution)/shard_map/while/body/eval_jaxpr/ppermute | solution.py:10
  382.9 9.8 %collective-permute-start = (f32[64,1024]{1,0:T(8,128)S(1)}, f32[64,1024]{1,0:T(8,128)S(1)}, u32[]{:S(2)}, u32[]{:S(2)}) collective-permute-start(f32[64,1024]{1,0:T(8,128)S(1)} %get-tuple-element.202), channel_id=1, source_target_pairs={{4,0},{8,4},{12,8},{16,12},{20,16},{24,20},{28,24},{32,28},{36,32}... | collective-permute-start | bytes 786440 | tf_op jit(solution)/shard_map/while/body/eval_jaxpr/ppermute | solution.py:10
  392.7 9.8 %collective-permute-start = (f32[64,1024]{1,0:T(8,128)S(1)}, f32[64,1024]{1,0:T(8,128)S(1)}, u32[]{:S(2)}, u32[]{:S(2)}) collective-permute-start(f32[64,1024]{1,0:T(8,128)S(1)} %get-tuple-element.202), channel_id=1, source_target_pairs={{4,0},{8,4},{12,8},{16,12},{20,16},{24,20},{28,24},{32,28},{36,32}... | collective-permute-start | bytes 786440 | tf_op jit(solution)/shard_map/while/body/eval_jaxpr/ppermute | solution.py:10
  402.5 9.8 %collective-permute-start = (f32[64,1024]{1,0:T(8,128)S(1)}, f32[64,1024]{1,0:T(8,128)S(1)}, u32[]{:S(2)}, u32[]{:S(2)}) collective-permute-start(f32[64,1024]{1,0:T(8,128)S(1)} %get-tuple-element.202), channel_id=1, source_target_pairs={{4,0},{8,4},{12,8},{16,12},{20,16},{24,20},{28,24},{32,28},{36,32}... | collective-permute-start | bytes 786440 | tf_op jit(solution)/shard_map/while/body/eval_jaxpr/ppermute | solution.py:10
  578.7 86.0 %collective-permute-start = (f32[64,1024]{1,0:T(8,128)S(1)}, f32[64,1024]{1,0:T(8,128)S(1)}, u32[]{:S(2)}, u32[]{:S(2)}) collective-permute-start(f32[64,1024]{1,0:T(8,128)S(1)} %get-tuple-element.202), channel_id=1, source_target_pairs={{4,0},{8,4},{12,8},{16,12},{20,16},{24,20},{28,24},{32,28},{36,32}... | collective-permute-start | bytes 786440 | tf_op jit(solution)/shard_map/while/body/eval_jaxpr/ppermute | solution.py:10
  (36 other events, 1641.5 us)
Sparse Core Ops, SparseCore 0:
  678.3 148.0 all-gather.2
